TPU v7x, 32 devices: a whole 2x2x4 slice. The times are simulated.
32 devices in a mesh: groups: 2 (over x), depth: 16 (over z, y, core).
Axes of the slice: x: 2, y: 2, z: 4, core: 2. Of those that a mesh axis runs over, the one named last changes fastest.
Arguments:
- fronts: bfloat16 [4, 64, 8, 2048], P(None, ('groups', 'depth')), parts along dimension 1, may hold values from -6 to 6
- extrap: bfloat16 [32, 16, 5, 2, 128, 128], P('depth'), may hold values from -0.15625 to 0.15625
- offsets: int32 [2, 5], replicated, may hold values from -2 to 2
- assign: int32 [2, 8], replicated, may hold values from 0 to 7, each once within a row
Outputs:
- images: float32 [8, 32, 2048], P(None, ('groups', 'depth')), parts along dimension 1
- last_fronts: bfloat16 [4, 64, 8, 2048], P(None, ('groups', 'depth')), parts along dimension 1
There are 2 independent parts, one for each index of `groups`. A program takes and returns all parts, laid end to end along the dimension named above; an argument that names none is the same for every part. Nothing has to cross between parts.
Inputs may be any that keep to these rules, and one draw needn't show every extreme that they name: `assign`: each row names every shot number once.
All inputs are finite; a program needn't handle non-finite values.
Results may differ from a plain program's by a relative error of at most 0.015.
Values may be sent and summed in bfloat16 or wider, within the bound.
A program may use at most 64 MiB of HBM per device.

v0:
```python
import functools
import math

import jax
import jax.numpy as jnp
from jax import lax
from jax.experimental import pallas as pl
from jax.experimental.pallas import tpu as pltpu
from jax.sharding import PartitionSpec as P

HANDOVERS = 8
PARTS = 4
VMEM_BYTES = 48 << 20
MESH = pl.DeviceIdType.MESH


def cuts(total, ends):
    edges = [0] + [e for e in ends if 0 < e < total] + [total]
    return list(zip(edges[:-1], edges[1:]))


def kernel(
    sections,
    owners,
    offsets_ref,
    assign_ref,
    fronts_hbm,
    extrap_ref,
    images_ref,
    last_ref,
    fronts_ref,
    oper,
    padded,
    outbox,
    inbox,
    half_image,
    slot_image,
    near_out,
    near_in,
    mate_out,
    mate_in,
    tail_out,
    tail_in,
    front_sem,
    load_sem,
    wave_send,
    wave_recv,
    near_send,
    near_recv,
    mate_send,
    mate_recv,
    tail_send,
    tail_recv,
):
    nfield, freqs, slots, _ = fronts_ref.shape
    nblk, band, block = extrap_ref.shape[1], extrap_ref.shape[2], extrap_ref.shape[-1]
    reach = band // 2
    half = owners // 2
    scale = 1.0 / math.sqrt(2.0 * freqs * owners)
    final = HANDOVERS - 1
    me = lax.axis_index("depth")
    depth = sections * owners
    section = me // owners
    owner = me % owners
    upper = owner // half
    lane = owner % half
    ahead = (me + owners) % depth
    behind = (me + depth - owners) % depth

    groups = cuts(nblk, (2, 8, 12))
    parts = cuts(nblk, (2, 8, 14))
    halves = cuts(nblk, (nblk // 2,))

    def front_load(freq):
        return pltpu.make_async_copy(
            fronts_hbm.at[:, freq], fronts_ref.at[:, freq], front_sem.at[freq]
        )

    def load(freq, part):
        lo, hi = groups[part]
        rows = pl.ds(lo, hi - lo)
        return pltpu.make_async_copy(
            extrap_ref.at[freq, rows], oper.at[freq, rows], load_sem.at[freq, part]
        )

    for freq in range(freqs):
        front_load(freq).start()
        for part in range(len(groups)):
            load(freq, part).start()

    def near(step):
        return section * owners + upper * half + (lane + step) % half

    def any_mate(step):
        return section * owners + (owner + step) % owners

    mate = section * owners + (owner + half) % owners
    barrier = pltpu.get_barrier_semaphore()
    greeted = [ahead] + ([behind] if sections > 2 else [])
    greeted = greeted + [any_mate(d) for d in range(1, owners)]
    for device in greeted:
        pl.semaphore_signal(barrier, inc=1, device_id={"depth": device}, device_id_type=MESH)

    offs = [offsets_ref[section, k] + reach for k in range(band)]
    slot_of = []
    for shot in range(slots):
        found = jnp.int32(0)
        for slot in range(slots):
            found = jnp.where(assign_ref[section, slot] == shot, slot, found)
        slot_of.append(found)

    def slot_for(target):
        chosen = slot_of[0]
        for shot in range(1, slots):
            chosen = jnp.where(target == shot, slot_of[shot], chosen)
        return chosen

    blank = jnp.zeros((reach,) + padded.shape[2:], padded.dtype)
    for freq in range(freqs):
        padded[freq, 0:reach] = blank
        padded[freq, reach + nblk : 2 * reach + nblk] = blank

    def unpack_front(freq):
        front_load(freq).wait()
        for b in range(nblk):
            cols = slice(b * block, (b + 1) * block)
            rows = [fronts_ref[c, freq, :, cols].astype(jnp.float32) for c in range(nfield)]
            padded[freq, reach + b] = jnp.concatenate(rows, axis=0).astype(padded.dtype)

    def remote(src, dst, send, recv, device):
        return pltpu.make_async_remote_copy(
            src_ref=src,
            dst_ref=dst,
            send_sem=send,
            recv_sem=recv,
            device_id={"depth": device},
            device_id_type=MESH,
        )

    def wave_copy(rnd, freq, part, lo, size):
        rows = pl.ds(lo, size)
        return remote(
            outbox.at[rnd, freq, rows],
            inbox.at[rnd, freq, rows],
            wave_send.at[rnd, freq, part],
            wave_recv.at[rnd, freq, part],
            ahead,
        )

    def near_copy(rnd, lo, size, device):
        rows = pl.ds(lo, size)
        return remote(
            near_out.at[rnd, rows],
            near_in.at[rnd, rows],
            near_send.at[rnd],
            near_recv.at[rnd],
            device,
        )

    def mate_copy(rnd):
        return remote(
            mate_out.at[rnd], mate_in.at[rnd], mate_send.at[rnd], mate_recv.at[rnd], mate
        )

    def tail_copy(piece, lo, size, device):
        rows = pl.ds(lo, size)
        return remote(
            tail_out.at[piece, rows],
            tail_in.at[piece, rows],
            tail_send.at[piece],
            tail_recv.at[piece],
            device,
        )

    def one_block(rnd, freq, b):
        lhs = jnp.concatenate([padded[freq, b + offs[k]] for k in range(band)], axis=1)
        rhs = jnp.concatenate(
            [
                jnp.concatenate([oper[freq, b, k, 0], oper[freq, b, k, 1]], axis=1)
                for k in range(band)
            ],
            axis=0,
        )
        both = jnp.dot(lhs, rhs, preferred_element_type=jnp.float32)
        re = [both[c * slots : (c + 1) * slots, :block] for c in range(nfield)]
        im = [both[c * slots : (c + 1) * slots, block:] for c in range(nfield)]
        new = [re[0] - im[1], im[0] + re[1], re[2] + im[3], re[3] - im[2]]
        rounded = jnp.concatenate(new, axis=0).astype(jnp.bfloat16)
        outbox[rnd, freq, b] = rounded
        wide = rounded.astype(jnp.float32)
        part = [wide[c * slots : (c + 1) * slots] for c in range(nfield)]
        image = part[0] * part[2] + part[1] * part[3]
        if freq > 0:
            image = image + half_image[b]
        if freq < freqs - 1:
            half_image[b] = image
        else:
            for slot in range(slots):
                slot_image[slot, pl.ds(b, 1), :] = image[slot : slot + 1] * scale

    def send_near(rnd):
        for step in range(half):
            column = (lane + step) % half
            near_out[rnd, step, 0] = slot_image[slot_for(upper * half + column)]
            near_out[rnd, step, 1] = slot_image[slot_for((1 - upper) * half + column)]
        for step in range(1, half):
            near_copy(rnd, step, 1, near(step)).start()

    def send_mate(rnd):
        near_copy(rnd, 1, half - 1, mate).wait_recv()
        mine = near_out[rnd, 0, 0]
        other = near_out[rnd, 0, 1]
        for step in range(1, half):
            mine = mine + near_in[rnd, step, 0]
            other = other + near_in[rnd, step, 1]
        images_ref[rnd] = mine
        mate_out[rnd] = other
        mate_copy(rnd).start()

    def finish_image(rnd):
        mate_copy(rnd).wait_recv()
        images_ref[rnd] = images_ref[rnd] + mate_in[rnd]

    def send_tail(piece):
        lo, hi = halves[piece]
        for step in range(owners):
            tail_out[piece, step] = slot_image[slot_for((owner + step) % owners), lo:hi]
        for step in range(1, owners):
            tail_copy(piece, step, 1, any_mate(step)).start()

    @pl.loop(0, HANDOVERS)
    def _(rnd):
        for freq in range(freqs):
            closing = freq == freqs - 1
            have = 0
            sent = 0
            imaged = 0
            for group, (lo, hi) in enumerate(groups):
                need = min(hi + reach, nblk)
                fresh = []
                while have < len(parts) and (parts[have][0] < need):
                    fresh.append(have)
                    have += 1

                @pl.when(rnd == 0)
                def _():
                    if group == 0:
                        unpack_front(freq)
                    load(freq, group).wait()

                @pl.when(rnd > 0)
                def _():
                    for part in fresh:
                        start, end = parts[part]
                        wave_copy(rnd - 1, freq, part, start, end - start).wait_recv()
                        padded[freq, reach + start : reach + end] = inbox[
                            rnd - 1, freq, start:end
                        ]

                for b in range(lo, hi):
                    one_block(rnd, freq, b)

                if freq == 0 and group == 0:

                    @pl.when(rnd == 0)
                    def _():
                        pl.semaphore_wait(barrier, len(greeted))

                outgoing = []
                while sent < len(parts) and parts[sent][1] <= hi:
                    outgoing.append(sent)
                    sent += 1

                @pl.when(rnd < final)
                def _():
                    for part in outgoing:
                        start, end = parts[part]
                        wave_copy(rnd, freq, part, start, end - start).start()

                @pl.when(rnd == final)
                def _():
                    nonlocal imaged
                    while closing and imaged < len(halves) and halves[imaged][1] <= hi:
                        send_tail(imaged)
                        imaged += 1
                    for b in range(lo, hi):
                        cols = slice(b * block, (b + 1) * block)
                        for c in range(nfield):
                            rows = slice(c * slots, (c + 1) * slots)
                            last_ref[c, freq, :, cols] = outbox[rnd, freq, b, rows, :]

            if freq == freqs - 2:

                @pl.when(rnd > 0)
                def _():
                    send_mate(rnd - 1)

        @pl.when(rnd < final)
        def _():
            send_near(rnd)

        @pl.when((rnd > 1) & (rnd < final))
        def _():
            finish_image(rnd - 2)

    @pl.loop(0, final)
    def _(rnd):
        for freq in range(freqs):
            for part, (lo, hi) in enumerate(parts):
                wave_copy(rnd, freq, part, lo, hi - lo).wait_send()
        near_copy(rnd, 1, half - 1, mate).wait_send()
        mate_copy(rnd).wait_send()

    finish_image(final - 2)
    finish_image(final - 1)
    for piece, (lo, hi) in enumerate(halves):
        tail_copy(piece, 1, owners - 1, mate).wait_recv()
        total = tail_out[piece, 0]
        for step in range(1, owners):
            total = total + tail_in[piece, step]
        images_ref[final, lo:hi] = total
    for piece in range(len(halves)):
        tail_copy(piece, 1, owners - 1, mate).wait_send()


def on_device(sections, owners, fronts, extrap, offsets, assign):
    nfield, freqs, slots, points = fronts.shape
    _, nblk, band, _, block, _ = extrap.shape
    moves = HANDOVERS - 1
    wave = (moves, freqs, nblk, nfield * slots, block)
    near = (moves, owners // 2, 2, nblk, block)
    mate = (moves, nblk, block)
    tail = (2, owners, nblk // 2, block)
    vmem = pl.BlockSpec(memory_space=pltpu.VMEM)
    smem = pl.BlockSpec(memory_space=pltpu.SMEM)
    hbm = pl.BlockSpec(memory_space=pltpu.HBM)
    dma = pltpu.SemaphoreType.DMA
    images, last = pl.pallas_call(
        functools.partial(kernel, sections, owners),
        out_shape=(
            jax.ShapeDtypeStruct((HANDOVERS, nblk, block), jnp.float32),
            jax.ShapeDtypeStruct(fronts.shape, fronts.dtype),
        ),
        in_specs=[smem, smem, hbm, hbm],
        out_specs=(vmem, vmem),
        scratch_shapes=[
            pltpu.VMEM(fronts.shape, fronts.dtype),
            pltpu.VMEM(extrap.shape, extrap.dtype),
            pltpu.VMEM((freqs, nblk + 2 * (band // 2), nfield * slots, block), fronts.dtype),
            pltpu.VMEM((HANDOVERS,) + wave[1:], fronts.dtype),
            pltpu.VMEM(wave, fronts.dtype),
            pltpu.VMEM((nblk, slots, block), jnp.float32),
            pltpu.VMEM((slots, nblk, block), jnp.float32),
            pltpu.VMEM(near, jnp.float32),
            pltpu.VMEM(near, jnp.float32),
            pltpu.VMEM(mate, jnp.float32),
            pltpu.VMEM(mate, jnp.float32),
            pltpu.VMEM(tail, jnp.float32),
            pltpu.VMEM(tail, jnp.float32),
            dma((freqs,)),
            dma((freqs, PARTS)),
            dma((moves, freqs, PARTS)),
            dma((moves, freqs, PARTS)),
            dma((moves,)),
            dma((moves,)),
            dma((moves,)),
            dma((moves,)),
            dma((2,)),
            dma((2,)),
        ],
        compiler_params=pltpu.CompilerParams(
            collective_id=0, has_side_effects=True, vmem_limit_bytes=VMEM_BYTES
        ),
    )(offsets, assign, fronts, extrap)
    return images.reshape(HANDOVERS, slots // owners, points), last


def solution(mesh):
    depth = mesh.shape["depth"]

    def program(fronts, extrap, offsets, assign):
        sections = offsets.shape[0]
        placed = (
            P(None, ("groups", "depth"), None, None),
            P("depth", None, None, None, None, None),
            P(),
            P(),
        )
        return jax.shard_map(
            functools.partial(on_device, sections, depth // sections),
            mesh=mesh,
            in_specs=placed,
            out_specs=(
                P(None, ("groups", "depth"), None),
                P(None, ("groups", "depth"), None, None),
            ),
            check_vma=False,
        )(fronts, extrap, offsets, assign)

    return program
```

profile of v0, /device:TPU:0, one launch (start us, length us, event | category | flops | bytes accessed | tf_op | source)
XLA Modules:
  0.0 96.3 jit_solution(4265124782929517481)
XLA Ops:
  0.6 0.0 copy-start
  0.6 0.9 copy-done
  1.6 0.0 copy-start.1
  1.6 0.7 copy-done.1
  2.3 0.0 copy-start.2
  2.3 0.7 copy-done.2
  2.9 92.0 %shard_map.59 = (f32[8,16,128]{2,1,0:T(8,128)S(1)}, bf16[4,2,8,2048]{3,2,1,0:T(8,128)(2,1)S(1)}) custom-call(s32[2,5]{1,0:T(2,128)S(1)} %copy-done.1, s32[2,8]{1,0:T(2,128)S(1)} %copy-done.2, bf16[4,2,8,2048]{3,2,1,0:T(8,128)(2,1)S(1)} %copy-done, bf16[2,16,5,2,128,128]{5,4,3,2,1,0:T(8,128)(2,1)} %extrap_ref.1), custom_call_target="tpu_custom_call" | custom-call | tf_op jit(solution)/shard_map/pallas_call | solution.py:338
  94.9 0.6 copy.9
  95.6 0.7 copy.10
Async XLA Ops:
  0.6 1.0 copy-start
  1.6 0.7 copy-start.1
  2.3 0.7 copy-start.2
where the time goes:
time: 96.5 us; the launch traced here: 96.3 us
  Pallas kernels  92 us (95%)
  local copies, waits for them, and re-layouts  3.63 us (4%)
    pallas_call x1, Pallas kernels, on_device(): pl.pallas_call(functools.partial(kernel, sections, owners), out_shape=(ja...  92 us
    unnamed x8, local copies, waits for them, and re-layouts  3.63 us

commit v1 on v0

v1 whole, which is shorter than its diff:
```python
import functools
import math

import jax
import jax.numpy as jnp
from jax import lax
from jax.experimental import pallas as pl
from jax.experimental.pallas import tpu as pltpu
from jax.sharding import PartitionSpec as P

HANDOVERS = 8
GROUP_ENDS = (2, 6, 12)
PART_ENDS = (2, 8, 14)
TAIL_ENDS = (8,)
LAG = 2
DEEP = 3
VMEM_BYTES = 48 << 20
STORE_BYTES = 1 << 20
MESH = pl.DeviceIdType.MESH


def cuts(total, ends):
    edges = [0] + [e for e in ends if 0 < e < total] + [total]
    return list(zip(edges[:-1], edges[1:]))


def kernel(
    sections,
    owners,
    offsets_hbm,
    assign_hbm,
    fronts_hbm,
    extrap_hbm,
    images_ref,
    last_ref,
    offsets_ref,
    assign_ref,
    fronts_ref,
    oper,
    padded,
    outbox,
    inbox,
    half_image,
    slot_image,
    share_out,
    share_in,
    table_sem,
    front_sem,
    load_sem,
    wave_send,
    wave_recv,
    share_send,
    share_recv,
):
    nfield, freqs, slots, _ = fronts_ref.shape
    nblk, band, block = oper.shape[1], oper.shape[2], oper.shape[-1]
    reach = band // 2
    scale = 1.0 / math.sqrt(2.0 * freqs * owners)
    final = HANDOVERS - 1
    me = lax.axis_index("depth")
    depth = sections * owners
    section = me // owners
    owner = me % owners
    ahead = (me + owners) % depth
    behind = (me + depth - owners) % depth

    groups = cuts(nblk, GROUP_ENDS)
    parts = cuts(nblk, PART_ENDS)
    tails = cuts(nblk, TAIL_ENDS)
    wave_slots = wave_send.shape[0]
    share_slots = 2 * LAG

    def any_mate(step):
        return section * owners + (owner + step) % owners

    barrier = pltpu.get_barrier_semaphore()
    greeted = [ahead] + ([behind] if sections > 2 else [])
    greeted = greeted + [any_mate(d) for d in range(1, owners)]
    for device in greeted:
        pl.semaphore_signal(barrier, inc=1, device_id={"depth": device}, device_id_type=MESH)

    offsets_load = pltpu.make_async_copy(offsets_hbm, offsets_ref, table_sem.at[0])
    assign_load = pltpu.make_async_copy(assign_hbm, assign_ref, table_sem.at[1])

    def front_load(freq):
        return pltpu.make_async_copy(
            fronts_hbm.at[:, freq], fronts_ref.at[:, freq], front_sem.at[freq]
        )

    def load(freq, part):
        lo, hi = groups[part]
        rows = pl.ds(lo, hi - lo)
        return pltpu.make_async_copy(
            extrap_hbm.at[freq, rows], oper.at[freq, rows], load_sem.at[freq, part]
        )

    queue = [(freq, part) for freq in range(freqs) for part in range(len(groups))]
    offsets_load.start()
    front_load(0).start()
    load(*queue[0]).start()
    assign_load.start()

    blank = jnp.zeros((reach,) + padded.shape[2:], padded.dtype)
    for freq in range(freqs):
        padded[freq, 0:reach] = blank
        padded[freq, reach + nblk : 2 * reach + nblk] = blank

    offsets_load.wait()
    assign_load.wait()
    for ahead_of in queue[1:DEEP]:
        load(*ahead_of).start()
    for freq in range(1, freqs):
        front_load(freq).start()
    offs = [offsets_ref[section, k] + reach for k in range(band)]
    slot_of = []
    for shot in range(slots):
        found = jnp.int32(0)
        for slot in range(slots):
            found = jnp.where(assign_ref[section, slot] == shot, slot, found)
        slot_of.append(found)

    def slot_for(target):
        chosen = slot_of[0]
        for shot in range(1, slots):
            chosen = jnp.where(target == shot, slot_of[shot], chosen)
        return chosen

    def unpack_front(freq):
        front_load(freq).wait()
        for b in range(nblk):
            cols = slice(b * block, (b + 1) * block)
            rows = [fronts_ref[c, freq, :, cols].astype(jnp.float32) for c in range(nfield)]
            padded[freq, reach + b] = jnp.concatenate(rows, axis=0).astype(padded.dtype)

    def remote(src, dst, send, recv, device):
        return pltpu.make_async_remote_copy(
            src_ref=src,
            dst_ref=dst,
            send_sem=send,
            recv_sem=recv,
            device_id={"depth": device},
            device_id_type=MESH,
        )

    def wave_copy(rnd, freq, part):
        lo, hi = parts[part]
        rows = pl.ds(lo, hi - lo)
        slot = rnd % wave_slots
        return remote(
            outbox.at[rnd, freq, rows],
            inbox.at[rnd, freq, rows],
            wave_send.at[slot, freq, part],
            wave_recv.at[slot, freq, part],
            ahead,
        )

    def share_copy(rnd, slot, lo, hi, step, count, device):
        rows = pl.ds(lo, hi - lo)
        return remote(
            share_out.at[rnd, pl.ds(step, count), rows],
            share_in.at[rnd, pl.ds(step, count), rows],
            share_send.at[slot],
            share_recv.at[slot],
            device,
        )

    def one_block(rnd, freq, b):
        lhs = jnp.concatenate([padded[freq, b + offs[k]] for k in range(band)], axis=1)
        rhs = jnp.concatenate(
            [
                jnp.concatenate([oper[freq, b, k, 0], oper[freq, b, k, 1]], axis=1)
                for k in range(band)
            ],
            axis=0,
        )
        both = jnp.dot(lhs, rhs, preferred_element_type=jnp.float32)
        re = [both[c * slots : (c + 1) * slots, :block] for c in range(nfield)]
        im = [both[c * slots : (c + 1) * slots, block:] for c in range(nfield)]
        new = [re[0] - im[1], im[0] + re[1], re[2] + im[3], re[3] - im[2]]
        rounded = jnp.concatenate(new, axis=0).astype(jnp.bfloat16)
        outbox[rnd, freq, b] = rounded
        wide = rounded.astype(jnp.float32)
        part = [wide[c * slots : (c + 1) * slots] for c in range(nfield)]
        image = part[0] * part[2] + part[1] * part[3]
        if freq > 0:
            image = image + half_image[b]
        if freq < freqs - 1:
            half_image[b] = image
        else:
            for slot in range(slots):
                slot_image[slot, pl.ds(b, 1), :] = image[slot : slot + 1] * scale

    def send_share(rnd, slot, lo, hi):
        for step in range(owners):
            share_out[rnd, step, lo:hi] = slot_image[slot_for((owner + step) % owners), lo:hi]
        for step in range(1, owners):
            share_copy(rnd, slot, lo, hi, step, 1, any_mate(step)).start()

    def finish_image(rnd, slot, lo, hi):
        share_copy(rnd, slot, lo, hi, 1, owners - 1, ahead).wait_recv()
        total = share_out[rnd, 0, lo:hi]
        for step in range(1, owners):
            total = total + share_in[rnd, step, lo:hi]
        images_ref[rnd, lo:hi] = total

    def drain_share(rnd, slot, lo, hi):
        share_copy(rnd, slot, lo, hi, 1, owners - 1, ahead).wait_send()

    def tail_slot(piece):
        return final % share_slots if piece == 0 else share_slots + piece - 1

    @pl.loop(0, HANDOVERS)
    def _(rnd):
        for freq in range(freqs):
            closing = freq == freqs - 1
            have = 0
            sent = 0
            shared = 0
            for group, (lo, hi) in enumerate(groups):
                need = min(hi + reach, nblk)
                fresh = []
                while have < len(parts) and (parts[have][0] < need):
                    fresh.append(have)
                    have += 1

                @pl.when(rnd == 0)
                def _():
                    if group == 0:
                        unpack_front(freq)
                    load(freq, group).wait()
                    for ahead_of in queue[freq * len(groups) + group :][DEEP : DEEP + 1]:
                        load(*ahead_of).start()

                @pl.when(rnd > 0)
                def _():
                    for part in fresh:
                        start, end = parts[part]
                        wave_copy(rnd - 1, freq, part).wait_recv()
                        padded[freq, reach + start : reach + end] = inbox[
                            rnd - 1, freq, start:end
                        ]

                for b in range(lo, hi):
                    one_block(rnd, freq, b)

                if freq == 0 and group == 0:

                    @pl.when(rnd == 0)
                    def _():
                        pl.semaphore_wait(barrier, len(greeted))

                outgoing = []
                while sent < len(parts) and parts[sent][1] <= hi:
                    outgoing.append(sent)
                    sent += 1

                if outgoing:

                    @pl.when((rnd >= wave_slots) & (rnd < final))
                    def _():
                        for part in outgoing:
                            wave_copy(rnd - wave_slots, freq, part).wait_send()

                    @pl.when(rnd < final)
                    def _():
                        for part in outgoing:
                            wave_copy(rnd, freq, part).start()

                @pl.when(rnd == final)
                def _():
                    nonlocal shared
                    while closing and shared < len(tails) and tails[shared][1] <= hi:
                        send_share(rnd, tail_slot(shared), *tails[shared])
                        shared += 1
                    for b in range(lo, hi):
                        cols = slice(b * block, (b + 1) * block)
                        for c in range(nfield):
                            rows = slice(c * slots, (c + 1) * slots)
                            last_ref[c, freq, :, cols] = outbox[rnd, freq, b, rows, :]

            if freq == 0:

                @pl.when(rnd >= LAG)
                def _():
                    before = rnd - LAG
                    finish_image(before, before % share_slots, 0, nblk)
                    drain_share(before, before % share_slots, 0, nblk)

        @pl.when(rnd < final)
        def _():
            send_share(rnd, rnd % share_slots, 0, nblk)

    for rnd in range(max(final - wave_slots, 0), final):
        for freq in range(freqs):
            for part in range(len(parts)):
                wave_copy(rnd, freq, part).wait_send()
    for rnd in range(max(HANDOVERS - LAG, 0), final):
        finish_image(rnd, rnd % share_slots, 0, nblk)
        drain_share(rnd, rnd % share_slots, 0, nblk)
    for piece, (lo, hi) in enumerate(tails):
        finish_image(final, tail_slot(piece), lo, hi)
    for piece, (lo, hi) in enumerate(tails):
        drain_share(final, tail_slot(piece), lo, hi)


def store(images_ref, last_ref, images_hbm, last_hbm, sem):
    copies = [
        pltpu.make_async_copy(last_ref, last_hbm, sem.at[0]),
        pltpu.make_async_copy(images_ref, images_hbm, sem.at[1]),
    ]
    for copy in copies:
        copy.start()
    for copy in copies:
        copy.wait()


def on_device(sections, owners, fronts, extrap, offsets, assign):
    nfield, freqs, slots, points = fronts.shape
    _, nblk, band, _, block, _ = extrap.shape
    moves = HANDOVERS - 1
    wave = (moves, freqs, nblk, nfield * slots, block)
    share = (HANDOVERS, owners, nblk, block)
    wave_slots = min(2 if sections == 2 else moves, moves)
    groups, parts, tails = (len(cuts(nblk, e)) for e in (GROUP_ENDS, PART_ENDS, TAIL_ENDS))
    vmem = pl.BlockSpec(memory_space=pltpu.VMEM)
    hbm = pl.BlockSpec(memory_space=pltpu.HBM)
    dma = pltpu.SemaphoreType.DMA
    shapes = (
        jax.ShapeDtypeStruct((HANDOVERS, nblk, block), jnp.float32),
        jax.ShapeDtypeStruct(fronts.shape, fronts.dtype),
    )
    held = [
        pltpu.with_memory_space_constraint(a, pltpu.HBM) for a in (offsets, assign, fronts, extrap)
    ]
    images, last = pl.pallas_call(
        functools.partial(kernel, sections, owners),
        out_shape=shapes,
        in_specs=[hbm] * 4,
        out_specs=(vmem, vmem),
        scratch_shapes=[
            pltpu.SMEM(offsets.shape, offsets.dtype),
            pltpu.SMEM(assign.shape, assign.dtype),
            pltpu.VMEM(fronts.shape, fronts.dtype),
            pltpu.VMEM(extrap.shape, extrap.dtype),
            pltpu.VMEM((freqs, nblk + 2 * (band // 2), nfield * slots, block), fronts.dtype),
            pltpu.VMEM((HANDOVERS,) + wave[1:], fronts.dtype),
            pltpu.VMEM(wave, fronts.dtype),
            pltpu.VMEM((nblk, slots, block), jnp.float32),
            pltpu.VMEM((slots, nblk, block), jnp.float32),
            pltpu.VMEM(share, jnp.float32),
            pltpu.VMEM(share, jnp.float32),
            dma((2,)),
            dma((freqs,)),
            dma((freqs, groups)),
            dma((wave_slots, freqs, parts)),
            dma((wave_slots, freqs, parts)),
            dma((2 * LAG + tails - 1,)),
            dma((2 * LAG + tails - 1,)),
        ],
        compiler_params=pltpu.CompilerParams(
            collective_id=0, has_side_effects=True, vmem_limit_bytes=VMEM_BYTES
        ),
    )(*held)
    images, last = pl.pallas_call(
        store,
        out_shape=shapes,
        in_specs=[vmem, vmem],
        out_specs=(hbm, hbm),
        scratch_shapes=[dma((2,))],
        compiler_params=pltpu.CompilerParams(vmem_limit_bytes=STORE_BYTES),
    )(images, last)
    return images.reshape(HANDOVERS, slots // owners, points), last


def solution(mesh):
    depth = mesh.shape["depth"]

    def program(fronts, extrap, offsets, assign):
        sections = offsets.shape[0]
        placed = (
            P(None, ("groups", "depth"), None, None),
            P("depth", None, None, None, None, None),
            P(),
            P(),
        )
        return jax.shard_map(
            functools.partial(on_device, sections, depth // sections),
            mesh=mesh,
            in_specs=placed,
            out_specs=(
                P(None, ("groups", "depth"), None),
                P(None, ("groups", "depth"), None, None),
            ),
            check_vma=False,
        )(fronts, extrap, offsets, assign)

    return program
```

time: 96.5 us -> 92.5 us (0.959)
  local copies, waits for them, and re-layouts: 3.63 us -> 0 us
    unnamed x8 -> x0, local copies, waits for them, and re-layouts: 3.63 us -> none
    pallas_call x1 -> x2, Pallas kernels: 92 us -> 91.7 us  [the longest x1 91 us: on_device(): pl.pallas_call(functools.partial(kernel, sections, owners), out_shape=sha...]
where the time goes in v1:
time: 92.5 us; the launch traced here: 92.3 us
  Pallas kernels  91.7 us (99%)
    pallas_call x1, Pallas kernels, on_device(): pl.pallas_call(functools.partial(kernel, sections, owners), out_shape=sha...  91 us

profile of v1, /device:TPU:0, one launch (start us, length us, event | category | flops | bytes accessed | tf_op | source)
XLA Modules:
  0.0 92.3 jit_solution(16726735891578282499)
XLA Ops:
  0.6 91.0 %shard_map.59 = (f32[8,16,128]{2,1,0:T(8,128)S(1)}, bf16[4,2,8,2048]{3,2,1,0:T(8,128)(2,1)S(1)}) custom-call(s32[2,5]{1,0:T(2,128)} %offsets_hbm.1, s32[2,8]{1,0:T(2,128)} %assign_hbm.1, bf16[4,2,8,2048]{3,2,1,0:T(8,128)(2,1)} %fronts_hbm.1, bf16[2,16,5,2,128,128]{5,4,3,2,1,0:T(8,128)(2,1)} %extrap_hbm.1), custom_call_target="tpu_custom_call" | custom-call | tf_op jit(solution)/shard_map/pallas_call | solution.py:335
  91.6 0.7 shard_map.60

commit v2 on v1

--- a/solution.py
+++ b/solution.py
@@ -9,11 +9,14 @@
 from jax.sharding import PartitionSpec as P
 
 HANDOVERS = 8
-GROUP_ENDS = (2, 6, 12)
-PART_ENDS = (2, 8, 14)
+GROUP_ENDS = (4, 8, 12)
+PART_ENDS = (4, 8, 12)
 TAIL_ENDS = (8,)
 LAG = 2
+WHERE = 0
 DEEP = 3
+SENDS = 1
+FIRST_ENDS = (1, 2)
 VMEM_BYTES = 48 << 20
 STORE_BYTES = 1 << 20
 MESH = pl.DeviceIdType.MESH
@@ -67,7 +70,8 @@
     groups = cuts(nblk, GROUP_ENDS)
     parts = cuts(nblk, PART_ENDS)
     tails = cuts(nblk, TAIL_ENDS)
-    wave_slots = wave_send.shape[0]
+    load_slots = load_sem.shape[0]
+    send_slots, wave_slots = wave_send.shape[0], wave_recv.shape[0]
     share_slots = 2 * LAG
 
     def any_mate(step):
@@ -87,18 +91,30 @@
             fronts_hbm.at[:, freq], fronts_ref.at[:, freq], front_sem.at[freq]
         )
 
-    def load(freq, part):
-        lo, hi = groups[part]
+    first = cuts(groups[0][1], FIRST_ENDS)
+    queue = [(0, lo, hi) for lo, hi in first] + [(0, lo, hi) for lo, hi in groups[1:]]
+    queue += [(freq, lo, hi) for freq in range(1, freqs) for lo, hi in groups]
+
+    def load(place):
+        freq, lo, hi = queue[place]
         rows = pl.ds(lo, hi - lo)
         return pltpu.make_async_copy(
-            extrap_hbm.at[freq, rows], oper.at[freq, rows], load_sem.at[freq, part]
-        )
-
-    queue = [(freq, part) for freq in range(freqs) for part in range(len(groups))]
+            extrap_hbm.at[freq, rows], oper.at[freq, rows], load_sem.at[place % load_slots]
+        )
+
+    def take(freq, lo, hi):
+        place = queue.index((freq, lo, hi))
+        load(place).wait()
+        if place + load_slots < len(queue):
+            load(place + load_slots).start()
+
     offsets_load.start()
     front_load(0).start()
-    load(*queue[0]).start()
+    for place in range(min(load_slots, len(queue))):
+        load(place).start()
     assign_load.start()
+    for freq in range(1, freqs):
+        front_load(freq).start()
 
     blank = jnp.zeros((reach,) + padded.shape[2:], padded.dtype)
     for freq in range(freqs):
@@ -106,23 +122,12 @@
         padded[freq, reach + nblk : 2 * reach + nblk] = blank
 
     offsets_load.wait()
-    assign_load.wait()
-    for ahead_of in queue[1:DEEP]:
-        load(*ahead_of).start()
-    for freq in range(1, freqs):
-        front_load(freq).start()
     offs = [offsets_ref[section, k] + reach for k in range(band)]
-    slot_of = []
-    for shot in range(slots):
-        found = jnp.int32(0)
+
+    def slot_for(target):
+        chosen = jnp.int32(0)
         for slot in range(slots):
-            found = jnp.where(assign_ref[section, slot] == shot, slot, found)
-        slot_of.append(found)
-
-    def slot_for(target):
-        chosen = slot_of[0]
-        for shot in range(1, slots):
-            chosen = jnp.where(target == shot, slot_of[shot], chosen)
+            chosen = jnp.where(assign_ref[section, slot] == target, slot, chosen)
         return chosen
 
     def unpack_front(freq):
@@ -142,15 +147,14 @@
             device_id_type=MESH,
         )
 
-    def wave_copy(rnd, freq, part):
-        lo, hi = parts[part]
+    def wave_copy(rnd, freq, part, some=None):
+        lo, hi = some or parts[part]
         rows = pl.ds(lo, hi - lo)
-        slot = rnd % wave_slots
         return remote(
             outbox.at[rnd, freq, rows],
             inbox.at[rnd, freq, rows],
-            wave_send.at[slot, freq, part],
-            wave_recv.at[slot, freq, part],
+            wave_send.at[rnd % send_slots, freq, part],
+            wave_recv.at[rnd % wave_slots, freq, part],
             ahead,
         )
 
@@ -223,13 +227,14 @@
                     fresh.append(have)
                     have += 1
 
+                opening = freq == 0 and group == 0
+
                 @pl.when(rnd == 0)
                 def _():
                     if group == 0:
                         unpack_front(freq)
-                    load(freq, group).wait()
-                    for ahead_of in queue[freq * len(groups) + group :][DEEP : DEEP + 1]:
-                        load(*ahead_of).start()
+                    if not opening:
+                        take(freq, lo, hi)
 
                 @pl.when(rnd > 0)
                 def _():
@@ -240,14 +245,24 @@
                             rnd - 1, freq, start:end
                         ]
 
-                for b in range(lo, hi):
-                    one_block(rnd, freq, b)
-
-                if freq == 0 and group == 0:
-
-                    @pl.when(rnd == 0)
-                    def _():
-                        pl.semaphore_wait(barrier, len(greeted))
+                for start, end in first if opening else [(lo, hi)]:
+                    if opening:
+
+                        @pl.when(rnd == 0)
+                        def _():
+                            take(freq, start, end)
+
+                    for b in range(start, end):
+                        one_block(rnd, freq, b)
+
+                    if opening:
+
+                        @pl.when(rnd == 0)
+                        def _():
+                            if start == 0:
+                                pl.semaphore_wait(barrier, len(greeted))
+                                assign_load.wait()
+                            wave_copy(rnd, freq, 0, (start, end)).start()
 
                 outgoing = []
                 while sent < len(parts) and parts[sent][1] <= hi:
@@ -256,12 +271,12 @@
 
                 if outgoing:
 
-                    @pl.when((rnd >= wave_slots) & (rnd < final))
+                    @pl.when((rnd >= send_slots) & (rnd < final))
                     def _():
                         for part in outgoing:
-                            wave_copy(rnd - wave_slots, freq, part).wait_send()
-
-                    @pl.when(rnd < final)
+                            wave_copy(rnd - send_slots, freq, part).wait_send()
+
+                    @pl.when((rnd >= int(opening)) & (rnd < final))
                     def _():
                         for part in outgoing:
                             wave_copy(rnd, freq, part).start()
@@ -278,7 +293,7 @@
                             rows = slice(c * slots, (c + 1) * slots)
                             last_ref[c, freq, :, cols] = outbox[rnd, freq, b, rows, :]
 
-            if freq == 0:
+            if freq == WHERE:
 
                 @pl.when(rnd >= LAG)
                 def _():
@@ -290,7 +305,7 @@
         def _():
             send_share(rnd, rnd % share_slots, 0, nblk)
 
-    for rnd in range(max(final - wave_slots, 0), final):
+    for rnd in range(max(final - send_slots, 0), final):
         for freq in range(freqs):
             for part in range(len(parts)):
                 wave_copy(rnd, freq, part).wait_send()
@@ -321,7 +336,8 @@
     wave = (moves, freqs, nblk, nfield * slots, block)
     share = (HANDOVERS, owners, nblk, block)
     wave_slots = min(2 if sections == 2 else moves, moves)
-    groups, parts, tails = (len(cuts(nblk, e)) for e in (GROUP_ENDS, PART_ENDS, TAIL_ENDS))
+    send_slots = SENDS or wave_slots
+    parts, tails = (len(cuts(nblk, e)) for e in (PART_ENDS, TAIL_ENDS))
     vmem = pl.BlockSpec(memory_space=pltpu.VMEM)
     hbm = pl.BlockSpec(memory_space=pltpu.HBM)
     dma = pltpu.SemaphoreType.DMA
@@ -351,8 +367,8 @@
             pltpu.VMEM(share, jnp.float32),
             dma((2,)),
             dma((freqs,)),
-            dma((freqs, groups)),
-            dma((wave_slots, freqs, parts)),
+            dma((DEEP,)),
+            dma((send_slots, freqs, parts)),
             dma((wave_slots, freqs, parts)),
             dma((2 * LAG + tails - 1,)),
             dma((2 * LAG + tails - 1,)),

time: 92.5 us -> 91.6 us (level)
  Pallas kernels: 91.7 us -> 90.7 us
    pallas_call x1, Pallas kernels: 91 us -> 90 us  [on_device(): pl.pallas_call(functools.partial(kernel, sections, owners), out_shape=sha...]
where the time goes in v2:
time: 91.6 us; the launch traced here: 91.4 us
  Pallas kernels  90.7 us (99%)
    pallas_call x1, Pallas kernels, on_device(): pl.pallas_call(functools.partial(kernel, sections, owners), out_shape=sha...  90 us

profile of v2, /device:TPU:0, one launch (start us, length us, event | category | flops | bytes accessed | tf_op | source)
XLA Modules:
  0.0 91.4 jit_solution(4004219461404075419)
XLA Ops:
  0.6 90.0 %shard_map.59 = (f32[8,16,128]{2,1,0:T(8,128)S(1)}, bf16[4,2,8,2048]{3,2,1,0:T(8,128)(2,1)S(1)}) custom-call(s32[2,5]{1,0:T(2,128)} %offsets_hbm.1, s32[2,8]{1,0:T(2,128)} %assign_hbm.1, bf16[4,2,8,2048]{3,2,1,0:T(8,128)(2,1)} %fronts_hbm.1, bf16[2,16,5,2,128,128]{5,4,3,2,1,0:T(8,128)(2,1)} %extrap_hbm.1), custom_call_target="tpu_custom_call" | custom-call | tf_op jit(solution)/shard_map/pallas_call | solution.py:351
  90.7 0.7 shard_map.60

commit v3 on v2

--- a/solution.py
+++ b/solution.py
@@ -9,7 +9,7 @@
 from jax.sharding import PartitionSpec as P
 
 HANDOVERS = 8
-GROUP_ENDS = (4, 8, 12)
+GROUP_ENDS = (4, 8, 10, 12)
 PART_ENDS = (4, 8, 12)
 TAIL_ENDS = (8,)
 LAG = 2

time: 91.6 us -> 91.7 us (level)
  no operation moved by 1% of the time
where the time goes in v3:
time: 91.7 us; the launch traced here: 91.6 us
  Pallas kernels  90.9 us (99%)
    pallas_call x1, Pallas kernels, on_device(): pl.pallas_call(functools.partial(kernel, sections, owners), out_shape=sha...  90.2 us

profile of v3, /device:TPU:0, one launch (start us, length us, event | category | flops | bytes accessed | tf_op | source)
XLA Modules:
  0.0 91.6 jit_solution(6965715897651456884)
XLA Ops:
  0.6 90.2 %shard_map.59 = (f32[8,16,128]{2,1,0:T(8,128)S(1)}, bf16[4,2,8,2048]{3,2,1,0:T(8,128)(2,1)S(1)}) custom-call(s32[2,5]{1,0:T(2,128)} %offsets_hbm.1, s32[2,8]{1,0:T(2,128)} %assign_hbm.1, bf16[4,2,8,2048]{3,2,1,0:T(8,128)(2,1)} %fronts_hbm.1, bf16[2,16,5,2,128,128]{5,4,3,2,1,0:T(8,128)(2,1)} %extrap_hbm.1), custom_call_target="tpu_custom_call" | custom-call | tf_op jit(solution)/shard_map/pallas_call | solution.py:351
  90.8 0.7 shard_map.60

commit v4 on v3

--- a/solution.py
+++ b/solution.py
@@ -11,7 +11,7 @@
 HANDOVERS = 8
 GROUP_ENDS = (4, 8, 10, 12)
 PART_ENDS = (4, 8, 12)
-TAIL_ENDS = (8,)
+TAIL_ENDS = ()
 LAG = 2
 WHERE = 0
 DEEP = 3

time: 91.7 us -> 91.7 us (level)
  no operation moved by 1% of the time
where the time goes in v4:
time: 91.7 us; the launch traced here: 91.5 us
  Pallas kernels  90.8 us (99%)
    pallas_call x1, Pallas kernels, on_device(): pl.pallas_call(functools.partial(kernel, sections, owners), out_shape=sha...  90.1 us

profile of v4, /device:TPU:0, one launch (start us, length us, event | category | flops | bytes accessed | tf_op | source)
XLA Modules:
  0.0 91.5 jit_solution(9892956874567084566)
XLA Ops:
  0.6 90.1 %shard_map.59 = (f32[8,16,128]{2,1,0:T(8,128)S(1)}, bf16[4,2,8,2048]{3,2,1,0:T(8,128)(2,1)S(1)}) custom-call(s32[2,5]{1,0:T(2,128)} %offsets_hbm.1, s32[2,8]{1,0:T(2,128)} %assign_hbm.1, bf16[4,2,8,2048]{3,2,1,0:T(8,128)(2,1)} %fronts_hbm.1, bf16[2,16,5,2,128,128]{5,4,3,2,1,0:T(8,128)(2,1)} %extrap_hbm.1), custom_call_target="tpu_custom_call" | custom-call | tf_op jit(solution)/shard_map/pallas_call | solution.py:351
  90.7 0.7 shard_map.60
